TPU v7x, 256 devices: a whole 4x4x8 slice. The times are simulated.
256 devices in a mesh: seq: 32 (over y, z_hi, x), grp: 8 (over z_lo, core).
Axes of the slice: x: 4, y: 4, z: 8 (z_hi: 2, z_lo: 4; z = z_hi * 4 + z_lo), core: 2. Of those that a mesh axis runs over, the one named last changes fastest.
Arguments:
- inputs: bfloat16 [4096, 8192], P('seq', 'grp'), may hold values from -10 to 10
- query_states: bfloat16 [4096, 8192], P('seq', 'grp'), may hold values from -12 to 12
- key_states: bfloat16 [4096, 1024], P('seq', 'grp'), may hold values from -6 to 6
- value_states: bfloat16 [4096, 1024], P('seq', 'grp'), may hold values from -6 to 6
- doc_ids: int32 [4096], replicated, may hold values from 0 to 7, never falling along the last dimension, each value on 1 to 3072 neighbouring positions
- modality: int32 [4096], P('seq'), may hold values from 0 to 1, as said below
- expert_ids: int32 [4096, 4], P('seq'), may hold values from -1 to 31, as said below
- norm_gain: float32 [8192], P('grp'), may hold values from 0.1 to 1.9
- router_w: bfloat16 [8192, 64], P('grp'), may hold values from -0.0625 to 0.0625
- w_in: bfloat16 [2, 32, 8192, 1408], P(None, 'seq', 'grp'), may hold values from -1 to 1
- w_out: bfloat16 [2, 32, 1408, 8192], P(None, 'seq', None, 'grp'), may hold values from -2 to 2
- grad_out: bfloat16 [4096, 8192], P('seq', 'grp'), may hold values from -12 to 12
Outputs:
- layer_out: bfloat16 [4096, 8192], P('seq', 'grp')
- state_grad: bfloat16 [4096, 8192], P('seq', 'grp')
Inputs may be any that keep to these rules, and one draw needn't show every extreme that they name: Modality is constant over aligned runs of 16 tokens; every block of 128 tokens held by one index of seq has a run of each modality. `expert_ids`: -1 marks an empty choice; the other entries of a token are distinct experts of its modality. At most 16 choices of the 128 tokens of one index of seq name one expert of one modality, and in every draw one text expert and one image expert are named by exactly 16 choices of every such block.
All inputs are finite; a program needn't handle non-finite values.
Results may differ from a plain program's by a relative error of at most 0.008.
Values may be sent and summed in bfloat16 or wider, within the bound.
A program may use at most 128 MiB of HBM per device.

v0:
```python
import jax
import jax.numpy as jnp
from jax import lax
from jax.sharding import PartitionSpec as P

D = 8192
HEADS = 64
KV_HEADS = 8
HEAD_DIM = 128
FF = 1408
TOP = 4
CAP = 16
eps_norm = 1e-05
gate_offset = 0.5


def gelu_back(pre_act, grad_in):
    return jax.vjp(lambda inner: jax.nn.gelu(inner, approximate=True), pre_act)[1](grad_in)[0]


def row_total(partial_value):
    return lax.psum(partial_value, "grp")


def dispatch(buffers):
    return lax.all_to_all(buffers, "seq", split_axis=1, concat_axis=1, tiled=True)


def collect(buffers):
    return lax.all_to_all(buffers, "seq", split_axis=1, concat_axis=1, tiled=True)


def hidden_step(partial_value, finish):
    summed = lax.psum(partial_value.astype(jnp.bfloat16), "grp").astype(jnp.float32)
    return finish(summed)


def attend(query_states, key_states, value_states, doc_ids):
    length = query_states.shape[0]
    kv_local = key_states.shape[1] // HEAD_DIM
    group_size = HEADS // KV_HEADS
    query_heads = query_states.reshape(length, kv_local, group_size, HEAD_DIM)
    first_query = lax.axis_index("seq") * length
    query_pos = first_query + jnp.arange(length, dtype=jnp.int32)
    query_doc = lax.dynamic_slice_in_dim(doc_ids, first_query, length)
    score_scale = HEAD_DIM ** (-0.5)
    key_piece = lax.all_gather(key_states, "seq", axis=0, tiled=True)
    value_piece = lax.all_gather(value_states, "seq", axis=0, tiled=True)
    piece_rows = key_piece.shape[0]
    best_score = jnp.full((length, kv_local, group_size), -1e30, jnp.float32)
    key_heads = key_piece.reshape(piece_rows, kv_local, HEAD_DIM)
    value_heads = value_piece.reshape(piece_rows, kv_local, HEAD_DIM).astype(jnp.float32)
    scores = (
        jnp.einsum("qhgd,khd->qhgk", query_heads, key_heads, preferred_element_type=jnp.float32)
        * score_scale
    )
    key_pos = jnp.arange(piece_rows, dtype=jnp.int32)
    allowed = (key_pos[None, :] <= query_pos[:, None]) & (doc_ids[None, :] == query_doc[:, None])
    allowed = allowed[:, None, None, :]
    scores = jnp.where(allowed, scores, -1e30)
    new_best = jnp.maximum(best_score, jnp.max(scores, axis=3))
    weights = jnp.where(allowed, jnp.exp(scores - new_best[..., None]), 0.0)
    totals = jnp.sum(weights, axis=3)
    summed = jnp.einsum("qhgk,khd->qhgd", weights, value_heads, precision=lax.Precision.HIGHEST)
    best_score, totals, summed = (new_best, totals, summed)
    return (
        (summed / totals[..., None])
        .reshape(length, kv_local * group_size * HEAD_DIM)
        .astype(jnp.bfloat16)
    )


def body(
    inputs,
    query_states,
    key_states,
    value_states,
    doc_ids,
    modality,
    expert_ids,
    norm_gain,
    router_w,
    w_in,
    w_out,
    grad_out,
):
    length, width_local = inputs.shape
    experts = lax.axis_size("seq")
    slot_total = 2 * experts * CAP
    attended = attend(query_states, key_states, value_states, doc_ids)
    resid_state = (inputs.astype(jnp.float32) + attended.astype(jnp.float32)).astype(jnp.bfloat16)
    state_wide = resid_state.astype(jnp.float32)
    squares = row_total(jnp.sum(state_wide * state_wide, axis=1))
    inv_rms = lax.rsqrt(squares / D + eps_norm)[:, None]
    scaled = state_wide * norm_gain[None, :]
    normed = (scaled * inv_rms).astype(jnp.bfloat16)
    logits = row_total(jnp.dot(normed, router_w, preferred_element_type=jnp.float32))
    kept_mask = expert_ids >= 0
    kept_wide = kept_mask.astype(jnp.float32)
    column = modality[:, None] * experts + jnp.where(kept_mask, expert_ids, 0)
    one_hot = (
        column[:, :, None] == jnp.arange(2 * experts, dtype=jnp.int32)[None, None, :]
    ) & kept_mask[:, :, None]
    chosen = jnp.sum(jnp.where(one_hot, logits[:, None, :], 0.0), axis=2)
    lifted = jax.nn.sigmoid(chosen)
    denominator = gate_offset + jnp.sum(kept_wide * lifted, axis=1, keepdims=True)
    gates = kept_wide * lifted / denominator
    entries = length * TOP
    flat_hot = one_hot.reshape(entries, 2 * experts).astype(jnp.bfloat16)
    entry_range = jnp.arange(entries, dtype=jnp.int32)
    earlier = (entry_range[:, None] > entry_range[None, :]).astype(jnp.bfloat16)
    before = jnp.dot(earlier, flat_hot, preferred_element_type=jnp.float32)
    slot_rank = jnp.sum(before * flat_hot.astype(jnp.float32), axis=1).astype(jnp.int32)
    slot_index = column.reshape(entries) * CAP + slot_rank
    table = (
        slot_index[:, None] == jnp.arange(slot_total, dtype=jnp.int32)[None, :]
    ) & kept_mask.reshape(entries)[:, None]
    table = table.astype(jnp.bfloat16).reshape(length, TOP, slot_total)
    token_table = jnp.sum(table, axis=1)
    w_in_local = w_in[:, 0]
    w_out_local = w_out[:, 0]
    sent_rows = jnp.einsum("ts,td->sd", token_table, normed, preferred_element_type=jnp.float32)
    sent_rows = sent_rows.astype(jnp.bfloat16).reshape(2, experts, CAP, width_local)
    got_rows = dispatch(sent_rows)
    partial_value = jnp.einsum(
        "ohn,ons->ohs",
        got_rows.reshape(2, experts * CAP, width_local),
        w_in_local,
        preferred_element_type=jnp.float32,
    ).reshape(2, experts, CAP, FF)

    def forward_finish(pre_act):
        return (jax.nn.gelu(pre_act, approximate=True).astype(jnp.bfloat16), pre_act)

    active, saved_pre = hidden_step(partial_value, forward_finish)
    expert_out = jnp.einsum(
        "nuv,nvg->nug",
        active.reshape(2, experts * CAP, FF),
        w_out_local,
        preferred_element_type=jnp.float32,
    ).astype(jnp.bfloat16)
    returned = collect(expert_out.reshape(2, experts, CAP, width_local)).reshape(
        slot_total, width_local
    )
    entry_out = jnp.einsum("tks,sd->tkd", table, returned, preferred_element_type=jnp.float32)
    mixture = jnp.sum(gates[:, :, None] * entry_out, axis=1)
    layer_out = (state_wide + mixture).astype(jnp.bfloat16)
    grad_wide = grad_out.astype(jnp.float32)
    gate_grad = row_total(jnp.sum(grad_wide[:, None, :] * entry_out, axis=2))
    gate_dot = jnp.sum(gates * gate_grad, axis=1, keepdims=True)
    logit_grad = kept_wide * (gate_grad - gate_dot) / denominator * lifted * (1.0 - lifted)
    logit_full = jnp.sum(jnp.where(one_hot, logit_grad[:, :, None], 0.0), axis=1)
    router_grad = jnp.dot(
        logit_full, router_w.astype(jnp.float32).T, precision=lax.Precision.HIGHEST
    )
    slot_gate = jnp.einsum(
        "tks,tk->s", table.astype(jnp.float32), gates, precision=lax.Precision.HIGHEST
    )
    grad_rows = (
        jnp.einsum("ts,td->sd", token_table, grad_out, preferred_element_type=jnp.float32)
        * slot_gate[:, None]
    )
    grad_rows = grad_rows.astype(jnp.bfloat16).reshape(2, experts, CAP, width_local)
    got_grads = dispatch(grad_rows)
    partial_back = jnp.einsum(
        "ukx,utx->ukt",
        got_grads.reshape(2, experts * CAP, width_local),
        w_out_local,
        preferred_element_type=jnp.float32,
    ).reshape(2, experts, CAP, FF)

    def backward_finish(act_grad):
        return (gelu_back(saved_pre, act_grad).astype(jnp.bfloat16), saved_pre)

    pre_grad = hidden_step(partial_back, backward_finish)[0]
    entry_grad = jnp.einsum(
        "upj,uoj->upo",
        pre_grad.reshape(2, experts * CAP, FF),
        w_in_local,
        preferred_element_type=jnp.float32,
    ).astype(jnp.bfloat16)
    grad_back = collect(entry_grad.reshape(2, experts, CAP, width_local)).reshape(
        slot_total, width_local
    )
    normed_grad = router_grad + jnp.einsum(
        "ts,sd->td", token_table, grad_back, preferred_element_type=jnp.float32
    )
    norm_dot = row_total(jnp.sum(normed_grad * scaled, axis=1))[:, None]
    state_grad = (
        grad_wide
        + inv_rms * norm_gain[None, :] * normed_grad
        - inv_rms**3 / D * state_wide * norm_dot
    )
    return (layer_out, state_grad.astype(jnp.bfloat16))


def solution(mesh):
    in_specs = (
        P("seq", "grp"),
        P("seq", "grp"),
        P("seq", "grp"),
        P("seq", "grp"),
        P(),
        P("seq"),
        P("seq", None),
        P("grp"),
        P("grp", None),
        P(None, "seq", "grp", None),
        P(None, "seq", None, "grp"),
        P("seq", "grp"),
    )
    out_specs = (P("seq", "grp"), P("seq", "grp"))
    return jax.shard_map(body, mesh=mesh, in_specs=in_specs, out_specs=out_specs, check_vma=False)
```

profile of v0, /device:TPU:1, one launch (start us, length us, event | category | flops | bytes accessed | tf_op | source)
XLA Modules:
  0.0 651.5 jit_solution(6634678139856003361)
XLA Ops:
  13.0 2.5 fusion.34
  15.5 79.9 %all-gather.3.cloned.1.call-done = bf16[4096,128]{1,0:T(8,128)(2,1)} async-done(((bf16[128,128]{1,0:T(8,128)(2,1)}), bf16[4096,128]{1,0:T(8,128)(2,1)}) %all-gather.3.cloned.1.call-update) | async-done | bytes 1048592 | tf_op jit(solution)/shard_map/all_gather | solution.py:47
  95.4 3.8 fusion.2
  99.2 5.7 copy-done.2
  104.9 4.0 fusion.3
  109.0 68.1 %all-gather.5.cloned.1.call-done = bf16[4096,128]{0,1:T(8,128)(2,1)} async-done(((bf16[128,128]{0,1:T(8,128)(2,1)}), bf16[4096,128]{0,1:T(8,128)(2,1)}) %all-gather.5.cloned.1.call-update) | async-done | bytes 1048592 | tf_op jit(solution)/shard_map/all_gather | solution.py:48
  177.2 12.9 %fusion.71 = f32[1,128,128,8]{2,1,3,0:T(8,128)S(1)} fusion(bf16[4096,128]{0,1:T(8,128)(2,1)} %all-gather.5.cloned.1.call-done, f32[4096,128,8]{1,0,2:T(8,128)} %copy-done.2, f32[128,8]{0,1:T(8,128)S(1)} %broadcast_maximum_fusion, pred[128,4096]{0,1:T(8,128)(4,1)S(1)} %fusion.34, f32[128,8]{0,1:T(8,128)S(1)} %fusion.3), kind=kOutput, calls=%fused_computation.69 | convolution fusion | flops 6459621376 | bytes 18882560 | tf_op jit(solution)/shard_map/qhgk,khd->qhgd/dot_general | solution.py:64
  190.5 15.0 %psum.42 = f32[128]{0:T(128)S(1)} all-reduce(f32[128]{0:T(128)S(1)} %get-tuple-element.6), channel_id=1, replica_groups=mesh['seq'=32,'grp'=8] {'grp'}, use_global_device_ids=true, to_apply=%region_3.4 | all-reduce | flops 128 | bytes 1024 | tf_op jit(solution)/shard_map/psum | solution.py:22
  205.8 22.5 %psum.43 = f32[128,64]{0,1:T(8,128)S(1)} all-reduce(f32[128,64]{0,1:T(8,128)S(1)} %fusion.92), channel_id=1, replica_groups=mesh['seq'=32,'grp'=8] {'grp'}, use_global_device_ids=true, to_apply=%region_4.5 | all-reduce | flops 8192 | bytes 65536 | tf_op jit(solution)/shard_map/psum | solution.py:22
  230.0 1.5 copy.86
  231.5 6.3 all-to-all-start.2
  238.6 1.5 copy.82
  240.1 47.7 %all-to-all-done.2 = bf16[2,32,16,1024]{3,2,0,1:T(8,128)(2,1)S(1)} async-done(((bf16[2,32,16,1024]{3,2,0,1:T(8,128)(2,1)}), bf16[2,32,16,1024]{3,2,0,1:T(8,128)(2,1)S(1)}, u32[]{:S(2)}, u32[]{:S(2)}) %all-to-all-start.2) | async-done | bytes 2097184 | tf_op jit(solution)/shard_map/all_to_all | solution.py:26
  287.8 8.5 %all-to-all-start = ((bf16[2,32,16,1024]{3,2,0,1:T(8,128)(2,1)}), bf16[2,32,16,1024]{3,2,0,1:T(8,128)(2,1)}, u32[]{:S(2)}, u32[]{:S(2)}) async-start(bf16[2,32,16,1024]{3,2,0,1:T(8,128)(2,1)} %copy.82), calls=%async_computation | async-start | bytes 4194304 | tf_op jit(solution)/shard_map/all_to_all | solution.py:26
  296.7 7.5 %fusion.31 = bf16[2,512,1408]{2,1,0:T(8,128)(2,1)} fusion(bf16[2,512,1024]{2,1,0:T(8,128)(2,1)S(1)} %bitcast.131, bf16[2,1,1408,1024]{3,2,1,0:T(8,128)(2,1)} %param.22), kind=kOutput, calls=%fused_computation.38 | convolution fusion | flops 2954231808 | bytes 10747904 | tf_op jit(solution)/shard_map/ukx,utx->ukt/dot_general | solution.py:165
  304.2 40.7 %all-to-all-done = bf16[2,32,16,1024]{3,2,0,1:T(8,128)(2,1)} async-done(((bf16[2,32,16,1024]{3,2,0,1:T(8,128)(2,1)}), bf16[2,32,16,1024]{3,2,0,1:T(8,128)(2,1)}, u32[]{:S(2)}, u32[]{:S(2)}) %all-to-all-start) | async-done | bytes 2097184 | tf_op jit(solution)/shard_map/all_to_all | solution.py:26
  344.8 1.8 copy.83
  346.7 7.4 %fusion.28 = bf16[2,512,1408]{2,1,0:T(8,128)(2,1)} fusion(bf16[2,512,1024]{2,1,0:T(8,128)(2,1)S(1)} %bitcast.132, bf16[2,1,1024,1408]{3,2,1,0:T(8,128)(2,1)} %param.21), kind=kOutput, calls=%fused_computation.37 | convolution fusion | flops 2954231808 | bytes 10747904 | tf_op jit(solution)/shard_map/ohn,ons->ohs/dot_general | solution.py:125
  354.1 135.9 %all-reduce.3.cloned.1.call-done = (bf16[2,32,16,1408]{3,2,1,0:T(8,128)(2,1)}, bf16[2,32,16,1408]{3,2,1,0:T(8,128)(2,1)}) async-done(((bf16[2,32,16,1408]{3,2,1,0:T(8,128)(2,1)}, bf16[2,32,16,1408]{3,2,1,0:T(8,128)(2,1)}), (bf16[2,32,16,1408]{3,2,1,0:T(8,128)(2,1)}, bf16[2,32,16,1408]{3,2,1,0:T(8,128)(2,1)})) %all-reduce.3.cloned.1.call-update) | async-done | bytes 5767184 | tf_op jit(solution)/shard_map/psum | solution.py:34
  490.0 7.6 %fusion.12 = (bf16[2,32,16,1408]{3,2,1,0:T(8,128)(2,1)}, bf16[2,32,16,1408]{3,2,1,0:T(8,128)(2,1)S(1)}) fusion(bf16[2,32,16,1408]{3,2,1,0:T(8,128)(2,1)} %get-tuple-element.5, bf16[2,32,16,1408]{3,2,1,0:T(8,128)(2,1)} %get-tuple-element.4), kind=kLoop, calls=%fused_computation.20 | loop fusion | flops 34603008 | bytes 11534336 | tf_op jit(solution)/shard_map/convert_element_type | solution.py:173
  497.6 3.7 fusion.46
  501.4 1.6 copy.84
  503.0 11.7 %all-to-all-start.1 = ((bf16[2,32,16,1024]{3,2,0,1:T(8,128)(2,1)}), bf16[2,32,16,1024]{3,2,0,1:T(8,128)(2,1)S(1)}, u32[]{:S(2)}, u32[]{:S(2)}) async-start(bf16[2,32,16,1024]{3,2,0,1:T(8,128)(2,1)} %copy.84), calls=%async_computation.1 | async-start | bytes 4194304 | tf_op jit(solution)/shard_map/all_to_all | solution.py:30
  514.6 7.0 %fusion.43 = bf16[2,512,1024]{2,1,0:T(8,128)(2,1)S(1)} fusion(bf16[2,512,1408]{2,1,0:T(8,128)(2,1)} %bitcast.128, bf16[2,1,1024,1408]{3,2,1,0:T(8,128)(2,1)} %param.21), kind=kOutput, calls=%fused_computation.51 | convolution fusion | flops 2953838592 | bytes 10747904 | tf_op jit(solution)/shard_map/upj,uoj->upo/dot_general | solution.py:176
  521.6 1.7 copy.88
  523.3 39.5 %all-to-all-done.1 = bf16[2,32,16,1024]{3,2,0,1:T(8,128)(2,1)S(1)} async-done(((bf16[2,32,16,1024]{3,2,0,1:T(8,128)(2,1)}), bf16[2,32,16,1024]{3,2,0,1:T(8,128)(2,1)S(1)}, u32[]{:S(2)}, u32[]{:S(2)}) %all-to-all-start.1) | async-done | bytes 2097184 | tf_op jit(solution)/shard_map/all_to_all | solution.py:30
  564.1 7.0 %all-to-all-start.3 = ((bf16[2,32,16,1024]{3,2,0,1:T(8,128)(2,1)}), bf16[2,32,16,1024]{3,2,0,1:T(8,128)(2,1)S(1)}, u32[]{:S(2)}, u32[]{:S(2)}) async-start(bf16[2,32,16,1024]{3,2,0,1:T(8,128)(2,1)} %copy.88), calls=%async_computation.3 | async-start | bytes 4194304 | tf_op jit(solution)/shard_map/all_to_all | solution.py:30
  571.1 1.8 copy.85
  572.9 2.2 multiply_reduce_fusion
  575.1 50.6 %psum.45 = f32[128,4]{0,1:T(4,128)S(1)} all-reduce(f32[128,4]{0,1:T(4,128)S(1)} %get-tuple-element.2), channel_id=1, replica_groups=mesh['seq'=32,'grp'=8] {'grp'}, use_global_device_ids=true, to_apply=%region_12.13 | all-reduce | flops 512 | bytes 4096 | tf_op jit(solution)/shard_map/psum | solution.py:22
  627.0 15.9 %psum.47 = f32[128]{0:T(128)S(1)} all-reduce(f32[128]{0:T(128)S(1)} %get-tuple-element.18), channel_id=1, replica_groups=mesh['seq'=32,'grp'=8] {'grp'}, use_global_device_ids=true, to_apply=%region_17.18 | all-reduce | flops 128 | bytes 1024 | tf_op jit(solution)/shard_map/psum | solution.py:22
  642.9 2.1 fusion.84
  (62 shorter events, 11.9 us)
Async XLA Ops:
  7.2 88.2 %copy-start = (bf16[128,1024]{1,0:T(8,128)(2,1)S(1)}, bf16[128,1024]{1,0:T(8,128)(2,1)}, u32[]{:S(2)}) copy-start(bf16[128,1024]{1,0:T(8,128)(2,1)} %param.13) | copy-start | bytes 786436
  7.2 88.2 %all-gather.3.cloned.1.call-start = ((), (), s32[]{:S(2)}) async-start(), calls=%async_computation.4 | async-start | bytes 1081344 | tf_op jit(solution)/shard_map/all_gather | solution.py:47
  7.9 169.2 %all-gather.5.cloned.1.call-start = ((), (), s32[]{:S(2)}) async-start(), calls=%async_computation.5 | async-start | bytes 1081344 | tf_op jit(solution)/shard_map/all_gather | solution.py:48
  99.2 5.7 copy-start.2
  109.0 81.3 %copy-start.5 = (bf16[128,1024]{1,0:T(8,128)(2,1)S(1)}, bf16[128,1024]{1,0:T(8,128)(2,1)}, u32[]{:S(2)}) copy-start(bf16[128,1024]{1,0:T(8,128)(2,1)} %param.12) | copy-start | bytes 786436
  109.0 96.5 %copy-start.6 = (bf16[1024,64]{0,1:T(8,128)(2,1)S(1)}, bf16[1024,64]{0,1:T(8,128)(2,1)}, u32[]{:S(2)}) copy-start(bf16[1024,64]{0,1:T(8,128)(2,1)} %param.20) | copy-start | bytes 393220
  109.0 96.5 %copy-start.7 = (f32[1024]{0:T(1024)S(1)}, f32[1024]{0:T(1024)}, u32[]{:S(2)}) copy-start(f32[1024]{0:T(1024)} %param.19) | copy-start | bytes 12292
  109.0 120.3 %copy-start.4 = (bf16[128,1024]{1,0:T(8,128)(2,1)S(1)}, bf16[128,1024]{1,0:T(8,128)(2,1)}, u32[]{:S(2)}) copy-start(bf16[128,1024]{1,0:T(8,128)(2,1)} %param.23) | copy-start | bytes 786436
  231.5 56.3 %all-to-all-start.2 = ((bf16[2,32,16,1024]{3,2,0,1:T(8,128)(2,1)}), bf16[2,32,16,1024]{3,2,0,1:T(8,128)(2,1)S(1)}, u32[]{:S(2)}, u32[]{:S(2)}) async-start(bf16[2,32,16,1024]{3,2,0,1:T(8,128)(2,1)} %copy.86), calls=%async_computation.2 | async-start | bytes 4194304 | tf_op jit(solution)/shard_map/all_to_all | solution.py:26
  287.8 57.0 %all-to-all-start = ((bf16[2,32,16,1024]{3,2,0,1:T(8,128)(2,1)}), bf16[2,32,16,1024]{3,2,0,1:T(8,128)(2,1)}, u32[]{:S(2)}, u32[]{:S(2)}) async-start(bf16[2,32,16,1024]{3,2,0,1:T(8,128)(2,1)} %copy.82), calls=%async_computation | async-start | bytes 4194304 | tf_op jit(solution)/shard_map/all_to_all | solution.py:26
  296.4 193.6 %all-reduce.3.cloned.1.call-start = ((), (), s32[]{:S(2)}) async-start(), calls=%async_computation.6 | async-start | bytes 11534336 | tf_op jit(solution)/shard_map/psum | solution.py:34
  354.1 143.5 %slice-start = ((s8[5767168]{0:T(1024)(128)(4,1)}), s8[1572864]{0:T(1024)(128)(4,1)S(1)}, s32[]{:S(2)}) async-start(s8[5767168]{0:T(1024)(128)(4,1)} %bitcast.138), calls=%async_computation.7 | async-start | bytes 3145728
  490.0 7.6 %slice-start.1 = ((s8[5767168]{0:T(1024)(128)(4,1)}), s8[4194304]{0:T(1024)(128)(4,1)S(1)}, s32[]{:S(2)}) async-start(s8[5767168]{0:T(1024)(128)(4,1)} %bitcast.138), calls=%async_computation.8 | async-start | bytes 8388608
  503.0 59.8 %all-to-all-start.1 = ((bf16[2,32,16,1024]{3,2,0,1:T(8,128)(2,1)}), bf16[2,32,16,1024]{3,2,0,1:T(8,128)(2,1)S(1)}, u32[]{:S(2)}, u32[]{:S(2)}) async-start(bf16[2,32,16,1024]{3,2,0,1:T(8,128)(2,1)} %copy.84), calls=%async_computation.1 | async-start | bytes 4194304 | tf_op jit(solution)/shard_map/all_to_all | solution.py:30
  562.8 1.3 copy-start.3
  564.1 61.7 %all-to-all-start.3 = ((bf16[2,32,16,1024]{3,2,0,1:T(8,128)(2,1)}), bf16[2,32,16,1024]{3,2,0,1:T(8,128)(2,1)S(1)}, u32[]{:S(2)}, u32[]{:S(2)}) async-start(bf16[2,32,16,1024]{3,2,0,1:T(8,128)(2,1)} %copy.88), calls=%async_computation.3 | async-start | bytes 4194304 | tf_op jit(solution)/shard_map/all_to_all | solution.py:30
  625.8 19.2 %copy-start.1 = (bf16[128,1024]{1,0:T(8,128)(2,1)S(1)}, bf16[128,1024]{1,0:T(8,128)(2,1)}, u32[]{:S(2)}) copy-start(bf16[128,1024]{1,0:T(8,128)(2,1)} %param.13) | copy-start | bytes 786436
Sparse Core Ops, SparseCore 0:
  11.4 83.9 all-gather.2
  99.2 77.9 all-gather.4
  354.2 135.7 all-reduce.2
where the time goes:
time: 652 us
  waiting for transfers between devices  413 us (63%)
  blocking collectives  104 us (16%)
  matrix products  48.5 us (7%)
  starting transfers between devices  33.5 us (5%)
  local copies, waits for them, and re-layouts  20.5 us (3%)
  other arithmetic  18.4 us (3%)
  between operations  14 us (2%)
    psum x1, waiting for transfers between devices, hidden_step(): lax.psum(partial_value.astype(jnp.bfloat16), 'grp').astype(jnp.float32)  136 us
    psum x4, blocking collectives, row_total(): return lax.psum(partial_value, 'grp')  104 us
    all_to_all x2, waiting for transfers between devices, dispatch(): lax.all_to_all(buffers, 'seq', split_axis=1, concat_axis=1, tiled=True)  88.4 us
    all_gather x1, waiting for transfers between devices, attend(): key_piece = lax.all_gather(key_states, 'seq', axis=0, tiled=True)  79.9 us
    all_gather x1, waiting for transfers between devices, attend(): value_piece = lax.all_gather(value_states, 'seq', axis=0, tiled=True)  68.1 us
    all_to_all x2, waiting for transfers between devices, collect(): lax.all_to_all(buffers, 'seq', split_axis=1, concat_axis=1, tiled=True)  39.5 us
    all_to_all x2, starting transfers between devices, collect(): lax.all_to_all(buffers, 'seq', split_axis=1, concat_axis=1, tiled=True)  18.6 us
    all_to_all x2, starting transfers between devices, dispatch(): lax.all_to_all(buffers, 'seq', split_axis=1, concat_axis=1, tiled=True)  14.8 us
  transfers between devices with their start and end apart: 7, of which 6 were waited for; matrix products, arithmetic and copies ran while one was open for 6% of the time, Pallas kernels for 0%

commit v1 on v0

--- a/solution.py
+++ b/solution.py
@@ -14,6 +14,12 @@
 gate_offset = 0.5
 
 
+def obtain_windows(view, frame_in):
+    part_next = jnp.concatenate([view, frame_in], axis=1)
+    mid_arr = lax.all_gather(part_next, "seq", axis=0, tiled=True)
+    return jnp.split(mid_arr, [view.shape[1]], 1)
+
+
 def gelu_back(pre_act, grad_in):
     return jax.vjp(lambda inner: jax.nn.gelu(inner, approximate=True), pre_act)[1](grad_in)[0]
 
@@ -44,8 +50,7 @@
     query_pos = first_query + jnp.arange(length, dtype=jnp.int32)
     query_doc = lax.dynamic_slice_in_dim(doc_ids, first_query, length)
     score_scale = HEAD_DIM ** (-0.5)
-    key_piece = lax.all_gather(key_states, "seq", axis=0, tiled=True)
-    value_piece = lax.all_gather(value_states, "seq", axis=0, tiled=True)
+    key_piece, value_piece = obtain_windows(key_states, value_states)
     piece_rows = key_piece.shape[0]
     best_score = jnp.full((length, kv_local, group_size), -1e30, jnp.float32)
     key_heads = key_piece.reshape(piece_rows, kv_local, HEAD_DIM)

time: 652 us -> 585 us (0.90)
  waiting for transfers between devices: 413 us -> 355 us
  local copies, waits for them, and re-layouts: 20.5 us -> 13.3 us
    all_gather x2 -> x1, waiting for transfers between devices: 148 us -> 91.4 us  [obtain_windows(): mid_arr = lax.all_gather(part_next, 'seq', axis=0, tiled=True)]
    unnamed x21 -> x20, local copies, waits for them, and re-layouts: 8.51 us -> 1.35 us
  transfers between devices with their start and end apart: 7 -> 6, of which waited for: 6 -> 5; matrix products, arithmetic and copies ran while one was open for 6% -> 5% of each run, Pallas kernels for 0% -> 0%
where the time goes in v1:
time: 585 us; the launch traced here: 584 us
  waiting for transfers between devices  355 us (61%)
  blocking collectives  105 us (18%)
  matrix products  45.1 us (8%)
  starting transfers between devices  31.9 us (5%)
  other arithmetic  20.1 us (3%)
  between operations  14.3 us (2%)
  local copies, waits for them, and re-layouts  13.3 us (2%)
    psum x1, waiting for transfers between devices, hidden_step(): lax.psum(partial_value.astype(jnp.bfloat16), 'grp').astype(jnp.float32)  136 us
    psum x4, blocking collectives, row_total(): return lax.psum(partial_value, 'grp')  105 us
    all_gather x1, waiting for transfers between devices, obtain_windows(): mid_arr = lax.all_gather(part_next, 'seq', axis=0, tiled=True)  91.4 us
    all_to_all x2, waiting for transfers between devices, dispatch(): lax.all_to_all(buffers, 'seq', split_axis=1, concat_axis=1, tiled=True)  88.4 us
    all_to_all x2, waiting for transfers between devices, collect(): lax.all_to_all(buffers, 'seq', split_axis=1, concat_axis=1, tiled=True)  39.3 us
    all_to_all x2, starting transfers between devices, collect(): lax.all_to_all(buffers, 'seq', split_axis=1, concat_axis=1, tiled=True)  18.9 us
    all_to_all x2, starting transfers between devices, dispatch(): lax.all_to_all(buffers, 'seq', split_axis=1, concat_axis=1, tiled=True)  12.9 us
  transfers between devices with their start and end apart: 6, of which 5 were waited for; matrix products, arithmetic and copies ran while one was open for 5% of the time, Pallas kernels for 0%

profile of v1, /device:TPU:1, one launch (start us, length us, event | category | flops | bytes accessed | tf_op | source)
XLA Modules:
  0.0 584.2 jit_solution(624936445112518706)
XLA Ops:
  7.2 1.4 pad_maximum_fusion
  12.3 2.5 fusion.34
  14.8 91.4 %all-gather.2.cloned.1.call-done = bf16[4096,256]{1,0:T(8,128)(2,1)} async-done(((bf16[128,256]{1,0:T(8,128)(2,1)}), bf16[4096,256]{1,0:T(8,128)(2,1)}) %all-gather.2.cloned.1.call-update) | async-done | bytes 2097168 | tf_op jit(solution)/shard_map/all_gather | solution.py:19
  106.1 3.8 fusion.2
  110.0 4.2 fusion.3
  114.3 9.5 %fusion.65 = f32[1,128,128,8]{2,1,3,0:T(8,128)S(1)} fusion(f32[4096,128,8]{1,0,2:T(8,128)S(1)} %get-tuple-element.17, f32[128,8]{0,1:T(8,128)S(1)} %broadcast_maximum_fusion, pred[128,4096]{0,1:T(8,128)(4,1)S(1)} %fusion.34, bf16[4096,256]{1,0:T(8,128)(2,1)S(1)} %copy-done.7, f32[128,8]{0,1:T(8,128)S(1)} %fusion.3), kind=kOutput, calls=%fused_computation.69 | convolution fusion | flops 6459621376 | bytes 18882560 | tf_op jit(solution)/shard_map/qhgk,khd->qhgd/dot_general | solution.py:69
  124.2 15.3 %psum.42 = f32[128]{0:T(128)S(1)} all-reduce(f32[128]{0:T(128)S(1)} %get-tuple-element.6), channel_id=1, replica_groups=mesh['seq'=32,'grp'=8] {'grp'}, use_global_device_ids=true, to_apply=%region_3.4 | all-reduce | flops 128 | bytes 1024 | tf_op jit(solution)/shard_map/psum | solution.py:28
  139.7 22.8 %psum.43 = f32[128,64]{0,1:T(8,128)S(1)} all-reduce(f32[128,64]{0,1:T(8,128)S(1)} %fusion.84), channel_id=1, replica_groups=mesh['seq'=32,'grp'=8] {'grp'}, use_global_device_ids=true, to_apply=%region_4.5 | all-reduce | flops 8192 | bytes 65536 | tf_op jit(solution)/shard_map/psum | solution.py:28
  164.2 1.5 copy.86
  165.8 4.4 all-to-all-start.2
  170.9 1.5 copy.82
  172.5 47.8 %all-to-all-done.2 = bf16[2,32,16,1024]{3,2,0,1:T(8,128)(2,1)S(1)} async-done(((bf16[2,32,16,1024]{3,2,0,1:T(8,128)(2,1)}), bf16[2,32,16,1024]{3,2,0,1:T(8,128)(2,1)S(1)}, u32[]{:S(2)}, u32[]{:S(2)}) %all-to-all-start.2) | async-done | bytes 2097184 | tf_op jit(solution)/shard_map/all_to_all | solution.py:32
  220.2 8.5 %all-to-all-start = ((bf16[2,32,16,1024]{3,2,0,1:T(8,128)(2,1)}), bf16[2,32,16,1024]{3,2,0,1:T(8,128)(2,1)}, u32[]{:S(2)}, u32[]{:S(2)}) async-start(bf16[2,32,16,1024]{3,2,0,1:T(8,128)(2,1)} %copy.82), calls=%async_computation | async-start | bytes 4194304 | tf_op jit(solution)/shard_map/all_to_all | solution.py:32
  229.1 7.5 %fusion.31 = bf16[2,512,1408]{2,1,0:T(8,128)(2,1)} fusion(bf16[2,512,1024]{2,1,0:T(8,128)(2,1)S(1)} %bitcast.129, bf16[2,1,1408,1024]{3,2,1,0:T(8,128)(2,1)} %param.22), kind=kOutput, calls=%fused_computation.38 | convolution fusion | flops 2954231808 | bytes 10747904 | tf_op jit(solution)/shard_map/ukx,utx->ukt/dot_general | solution.py:170
  236.6 40.7 %all-to-all-done = bf16[2,32,16,1024]{3,2,0,1:T(8,128)(2,1)} async-done(((bf16[2,32,16,1024]{3,2,0,1:T(8,128)(2,1)}), bf16[2,32,16,1024]{3,2,0,1:T(8,128)(2,1)}, u32[]{:S(2)}, u32[]{:S(2)}) %all-to-all-start) | async-done | bytes 2097184 | tf_op jit(solution)/shard_map/all_to_all | solution.py:32
  277.2 1.8 copy.83
  279.1 7.4 %fusion.28 = bf16[2,512,1408]{2,1,0:T(8,128)(2,1)} fusion(bf16[2,512,1024]{2,1,0:T(8,128)(2,1)S(1)} %bitcast.130, bf16[2,1,1024,1408]{3,2,1,0:T(8,128)(2,1)} %param.21), kind=kOutput, calls=%fused_computation.37 | convolution fusion | flops 2954231808 | bytes 10747904 | tf_op jit(solution)/shard_map/ohn,ons->ohs/dot_general | solution.py:130
  286.5 135.9 %all-reduce.3.cloned.1.call-done = (bf16[2,32,16,1408]{3,2,1,0:T(8,128)(2,1)}, bf16[2,32,16,1408]{3,2,1,0:T(8,128)(2,1)}) async-done(((bf16[2,32,16,1408]{3,2,1,0:T(8,128)(2,1)}, bf16[2,32,16,1408]{3,2,1,0:T(8,128)(2,1)}), (bf16[2,32,16,1408]{3,2,1,0:T(8,128)(2,1)}, bf16[2,32,16,1408]{3,2,1,0:T(8,128)(2,1)})) %all-reduce.3.cloned.1.call-update) | async-done | bytes 5767184 | tf_op jit(solution)/shard_map/psum | solution.py:40
  422.4 7.6 %fusion.12 = (bf16[2,32,16,1408]{3,2,1,0:T(8,128)(2,1)}, bf16[2,32,16,1408]{3,2,1,0:T(8,128)(2,1)S(1)}) fusion(bf16[2,32,16,1408]{3,2,1,0:T(8,128)(2,1)} %get-tuple-element.5, bf16[2,32,16,1408]{3,2,1,0:T(8,128)(2,1)} %get-tuple-element.4), kind=kLoop, calls=%fused_computation.20 | loop fusion | flops 34603008 | bytes 11534336 | tf_op jit(solution)/shard_map/convert_element_type | solution.py:178
  430.0 3.7 fusion.46
  433.8 1.6 copy.84
  435.4 11.9 %all-to-all-start.1 = ((bf16[2,32,16,1024]{3,2,0,1:T(8,128)(2,1)}), bf16[2,32,16,1024]{3,2,0,1:T(8,128)(2,1)S(1)}, u32[]{:S(2)}, u32[]{:S(2)}) async-start(bf16[2,32,16,1024]{3,2,0,1:T(8,128)(2,1)} %copy.84), calls=%async_computation.1 | async-start | bytes 4194304 | tf_op jit(solution)/shard_map/all_to_all | solution.py:36
  447.3 7.0 %fusion.43 = bf16[2,512,1024]{2,1,0:T(8,128)(2,1)S(1)} fusion(bf16[2,512,1408]{2,1,0:T(8,128)(2,1)} %bitcast.126, bf16[2,1,1024,1408]{3,2,1,0:T(8,128)(2,1)} %param.21), kind=kOutput, calls=%fused_computation.51 | convolution fusion | flops 2953838592 | bytes 10747904 | tf_op jit(solution)/shard_map/upj,uoj->upo/dot_general | solution.py:181
  454.3 1.7 copy.88
  455.9 39.3 %all-to-all-done.1 = bf16[2,32,16,1024]{3,2,0,1:T(8,128)(2,1)S(1)} async-done(((bf16[2,32,16,1024]{3,2,0,1:T(8,128)(2,1)}), bf16[2,32,16,1024]{3,2,0,1:T(8,128)(2,1)S(1)}, u32[]{:S(2)}, u32[]{:S(2)}) %all-to-all-start.1) | async-done | bytes 2097184 | tf_op jit(solution)/shard_map/all_to_all | solution.py:36
  495.3 1.3 copy-done.2
  496.5 6.9 %all-to-all-start.3 = ((bf16[2,32,16,1024]{3,2,0,1:T(8,128)(2,1)}), bf16[2,32,16,1024]{3,2,0,1:T(8,128)(2,1)S(1)}, u32[]{:S(2)}, u32[]{:S(2)}) async-start(bf16[2,32,16,1024]{3,2,0,1:T(8,128)(2,1)} %copy.88), calls=%async_computation.3 | async-start | bytes 4194304 | tf_op jit(solution)/shard_map/all_to_all | solution.py:36
  503.5 1.8 copy.85
  505.3 2.2 multiply_reduce_fusion
  507.5 50.6 %psum.45 = f32[128,4]{0,1:T(4,128)S(1)} all-reduce(f32[128,4]{0,1:T(4,128)S(1)} %get-tuple-element.2), channel_id=1, replica_groups=mesh['seq'=32,'grp'=8] {'grp'}, use_global_device_ids=true, to_apply=%region_12.13 | all-reduce | flops 512 | bytes 4096 | tf_op jit(solution)/shard_map/psum | solution.py:28
  559.4 15.9 %psum.47 = f32[128]{0:T(128)S(1)} all-reduce(f32[128]{0:T(128)S(1)} %get-tuple-element.18), channel_id=1, replica_groups=mesh['seq'=32,'grp'=8] {'grp'}, use_global_device_ids=true, to_apply=%region_17.18 | all-reduce | flops 128 | bytes 1024 | tf_op jit(solution)/shard_map/psum | solution.py:28
  575.3 2.1 fusion.76
  (59 shorter events, 8.4 us)
Async XLA Ops:
  7.2 99.0 %copy-start = (bf16[128,1024]{1,0:T(8,128)(2,1)S(1)}, bf16[128,1024]{1,0:T(8,128)(2,1)}, u32[]{:S(2)}) copy-start(bf16[128,1024]{1,0:T(8,128)(2,1)} %param.13) | copy-start | bytes 786436
  7.2 99.0 %all-gather.2.cloned.1.call-start = ((), (), s32[]{:S(2)}) async-start(), calls=%async_computation.4 | async-start | bytes 2162688 | tf_op jit(solution)/shard_map/all_gather | solution.py:19
  110.0 4.3 copy-start.7
  114.2 9.8 %copy-start.4 = (bf16[128,1024]{1,0:T(8,128)(2,1)S(1)}, bf16[128,1024]{1,0:T(8,128)(2,1)}, u32[]{:S(2)}) copy-start(bf16[128,1024]{1,0:T(8,128)(2,1)} %param.12) | copy-start | bytes 786436
  114.2 25.2 %copy-start.5 = (bf16[1024,64]{0,1:T(8,128)(2,1)S(1)}, bf16[1024,64]{0,1:T(8,128)(2,1)}, u32[]{:S(2)}) copy-start(bf16[1024,64]{0,1:T(8,128)(2,1)} %param.20) | copy-start | bytes 393220
  114.2 25.2 %copy-start.6 = (f32[1024]{0:T(1024)S(1)}, f32[1024]{0:T(1024)}, u32[]{:S(2)}) copy-start(f32[1024]{0:T(1024)} %param.19) | copy-start | bytes 12292
  114.3 49.2 %copy-start.3 = (bf16[128,1024]{1,0:T(8,128)(2,1)S(1)}, bf16[128,1024]{1,0:T(8,128)(2,1)}, u32[]{:S(2)}) copy-start(bf16[128,1024]{1,0:T(8,128)(2,1)} %param.23) | copy-start | bytes 786436
  165.8 54.5 %all-to-all-start.2 = ((bf16[2,32,16,1024]{3,2,0,1:T(8,128)(2,1)}), bf16[2,32,16,1024]{3,2,0,1:T(8,128)(2,1)S(1)}, u32[]{:S(2)}, u32[]{:S(2)}) async-start(bf16[2,32,16,1024]{3,2,0,1:T(8,128)(2,1)} %copy.86), calls=%async_computation.2 | async-start | bytes 4194304 | tf_op jit(solution)/shard_map/all_to_all | solution.py:32
  220.2 57.0 %all-to-all-start = ((bf16[2,32,16,1024]{3,2,0,1:T(8,128)(2,1)}), bf16[2,32,16,1024]{3,2,0,1:T(8,128)(2,1)}, u32[]{:S(2)}, u32[]{:S(2)}) async-start(bf16[2,32,16,1024]{3,2,0,1:T(8,128)(2,1)} %copy.82), calls=%async_computation | async-start | bytes 4194304 | tf_op jit(solution)/shard_map/all_to_all | solution.py:32
  228.7 193.6 %all-reduce.3.cloned.1.call-start = ((), (), s32[]{:S(2)}) async-start(), calls=%async_computation.5 | async-start | bytes 11534336 | tf_op jit(solution)/shard_map/psum | solution.py:40
  286.5 143.5 %slice-start = ((s8[5767168]{0:T(1024)(128)(4,1)}), s8[1572864]{0:T(1024)(128)(4,1)S(1)}, s32[]{:S(2)}) async-start(s8[5767168]{0:T(1024)(128)(4,1)} %bitcast.136), calls=%async_computation.6 | async-start | bytes 3145728
  422.4 7.6 %slice-start.1 = ((s8[5767168]{0:T(1024)(128)(4,1)}), s8[4194304]{0:T(1024)(128)(4,1)S(1)}, s32[]{:S(2)}) async-start(s8[5767168]{0:T(1024)(128)(4,1)} %bitcast.136), calls=%async_computation.7 | async-start | bytes 8388608
  435.4 59.9 %all-to-all-start.1 = ((bf16[2,32,16,1024]{3,2,0,1:T(8,128)(2,1)}), bf16[2,32,16,1024]{3,2,0,1:T(8,128)(2,1)S(1)}, u32[]{:S(2)}, u32[]{:S(2)}) async-start(bf16[2,32,16,1024]{3,2,0,1:T(8,128)(2,1)} %copy.84), calls=%async_computation.1 | async-start | bytes 4194304 | tf_op jit(solution)/shard_map/all_to_all | solution.py:36
  495.3 1.3 copy-start.2
  496.5 61.6 %all-to-all-start.3 = ((bf16[2,32,16,1024]{3,2,0,1:T(8,128)(2,1)}), bf16[2,32,16,1024]{3,2,0,1:T(8,128)(2,1)S(1)}, u32[]{:S(2)}, u32[]{:S(2)}) async-start(bf16[2,32,16,1024]{3,2,0,1:T(8,128)(2,1)} %copy.88), calls=%async_computation.3 | async-start | bytes 4194304 | tf_op jit(solution)/shard_map/all_to_all | solution.py:36
  558.2 19.2 %copy-start.1 = (bf16[128,1024]{1,0:T(8,128)(2,1)S(1)}, bf16[128,1024]{1,0:T(8,128)(2,1)}, u32[]{:S(2)}) copy-start(bf16[128,1024]{1,0:T(8,128)(2,1)} %param.13) | copy-start | bytes 786436
Sparse Core Ops, SparseCore 0:
  12.1 93.9 all-gather.1
  286.6 135.7 all-reduce.2
